TPU v7x, 512 devices: a whole 4x8x8 slice. The times are simulated.
512 devices in a mesh: blk: 32 (over z_lo, y, core), rows: 16 (over x, z_hi).
Axes of the slice: x: 4, y: 8, z: 8 (z_hi: 4, z_lo: 2; z = z_hi * 2 + z_lo), core: 2. Of those that a mesh axis runs over, the one named last changes fastest.
Arguments:
- covariance: float32 [16384, 2, 32, 256], P('rows', None, 'blk'), may hold values from 0 to 5, as said below
- panel_order: int32 [64], replicated, may hold values from 0 to 63, each once
Outputs:
- factored: float32 [16384, 2, 32, 256], P('rows', None, 'blk')
Inputs may be any that keep to these rules, and one draw needn't show every extreme that they name: covariance is symmetric and positive definite. `panel_order`: every panel appears once; panel j is held by index j % 32 of blk.
All inputs are finite; a program needn't handle non-finite values.
Results may differ from a plain program's by a relative error of at most 0.0003.
Values sent between devices are 32-bit elements; how exact they have to be, the bound alone decides.
No kernel may reach another device: no remote copies, remote signals or barrier semaphores. Data moves between devices by JAX's collectives and lax.ppermute only.
A program may use at most 64 MiB of HBM per device.

v0:
```python
import jax
import jax.numpy as jnp
from jax import lax
from jax.sharding import PartitionSpec as P

SECTIONS = 2


def padded_to(lines, size):
    spare = -lines.shape[0] % size
    if not spare:
        return lines
    return jnp.concatenate([lines, jnp.zeros((spare, *lines.shape[1:]), lines.dtype)])


def broadcast_by_parts(array, axis, root):
    lines = jnp.where(lax.axis_index(axis) == root, array, jnp.zeros_like(array)).reshape(
        -1, *array.shape[1:][-1:]
    )
    padded = padded_to(lines, lax.axis_size(axis))
    own = lax.psum_scatter(padded, axis, scatter_dimension=0, tiled=True)
    return lax.all_gather(own, axis, axis=0, tiled=True)[: len(lines)].reshape(array.shape)


def from_root(array, axis, root):
    return lax.dynamic_index_in_dim(lax.all_gather(array, axis), root, 0, keepdims=False)


def inverse_factor(diagonal_block):
    lower_factor = jnp.linalg.cholesky(diagonal_block)
    identity_block = jnp.eye(diagonal_block.shape[0], dtype=diagonal_block.dtype)
    return lax.linalg.triangular_solve(lower_factor, identity_block, left_side=True, lower=True)


def product(first_matrix, second_matrix):
    return jnp.dot(
        first_matrix,
        second_matrix,
        precision=lax.Precision.HIGHEST,
        preferred_element_type=jnp.float32,
    )


def local(covariance, panel_order):
    row_count = covariance.shape[0]
    slot_count = covariance.shape[1]
    panel_width = covariance.shape[3]
    owner_count = lax.axis_size("blk")
    column_index = lax.axis_index("blk")
    row_index = lax.axis_index("rows")
    working = covariance.reshape(row_count, slot_count, panel_width)
    identity_block = jnp.eye(panel_width, dtype=jnp.float32)
    slot_panels = jnp.arange(slot_count, dtype=jnp.int32) * owner_count + column_index
    for round_index in range(SECTIONS):
        target = panel_order[round_index]
        owner_column = target % owner_count
        slot_here = target // owner_count
        first_column = target * panel_width
        root_row = first_column // row_count
        offset = first_column % row_count
        finished = jnp.any(slot_panels[:, None] == panel_order[None, : round_index + 1], axis=1)
        target_slot = slot_panels == target
        live_weight = jnp.where(finished, 0.0, 1.0).astype(jnp.float32)
        local_panel = lax.dynamic_index_in_dim(working, slot_here, 1, keepdims=False)
        received_panel = broadcast_by_parts(local_panel, "blk", owner_column)
        diagonal_block = lax.dynamic_slice_in_dim(received_panel, offset, panel_width, 0)
        diagonal_block = jnp.where(row_index == root_row, diagonal_block, identity_block)
        inverse = inverse_factor(diagonal_block)
        across = lax.dynamic_slice_in_dim(working, offset, panel_width, 0).reshape(
            panel_width, slot_count * panel_width
        )
        solved = product(inverse.T, product(inverse, across)).reshape(
            panel_width, slot_count, panel_width
        )
        solved = jnp.where(
            target_slot[None, :, None], inverse.T[:, None, :], solved * live_weight[None, :, None]
        )
        solved = from_root(solved, "rows", root_row)
        change = jnp.einsum(
            "rk,kpc->rpc",
            received_panel,
            solved,
            precision=lax.Precision.HIGHEST,
            preferred_element_type=jnp.float32,
        )
        working = jnp.where(target_slot[None, :, None], change, working - change)
    return working.reshape(row_count, slot_count, 1, panel_width)


def solution(mesh):
    return jax.shard_map(
        local,
        mesh=mesh,
        in_specs=(P("rows", None, "blk", None), P()),
        out_specs=P("rows", None, "blk", None),
        check_vma=False,
    )
```

profile of v0, /device:TPU:2, one launch (start us, length us, event | category | flops | bytes accessed | tf_op | source)
XLA Modules:
  0.0 798.5 jit_solution(15428723638569665150)
XLA Ops:
  10.4 1.9 constant_dynamic-slice_fusion.5
  15.2 125.6 %reduce-scatter.7.cloned.1.call-done = f32[32,256]{1,0:T(8,128)} async-done(((f32[1024,256]{1,0:T(8,128)}), f32[32,256]{1,0:T(8,128)}) %reduce-scatter.7.cloned.1.call-update) | async-done | bytes 32784 | tf_op jit(solution)/shard_map/reduce_scatter | solution.py:21
  141.6 1.6 dynamic-slice_reduce_fusion
  143.9 60.9 %all-gather.5.cloned.1.call-done = f32[1024,256]{1,0:T(8,128)} async-done(((f32[32,256]{1,0:T(8,128)}), f32[1024,256]{1,0:T(8,128)}) %all-gather.5.cloned.1.call-update) | async-done | bytes 1048592 | tf_op jit(solution)/shard_map/all_gather | solution.py:22
  208.5 11.7 %cholesky.130 = f32[128,128]{1,0:T(8,128)S(1)} custom-call(f32[128,128]{1,0:T(8,128)S(1)} %cholesky.194), custom_call_target="Cholesky" | custom-call | tf_op jit(solution)/shard_map/jit(cholesky)/cholesky | solution.py:30
  220.2 9.8 %custom-call.13 = f32[1,128,128]{1,2,0:T(8,128)S(1)} custom-call(f32[1,128,128]{2,1,0:T(8,128)S(1)} %get-tuple-element.52), custom_call_target="InvertDiagBlocksLowerTriangular" | custom-call | tf_op jit(solution)/shard_map/jit(cholesky)/cholesky | solution.py:30
  232.2 11.9 %cholesky.147 = f32[128,128]{1,0:T(8,128)S(1)} custom-call(f32[128,128]{1,0:T(8,128)S(1)} %convolution_subtract_fusion.3), custom_call_target="Cholesky" | custom-call | tf_op jit(solution)/shard_map/jit(cholesky)/cholesky | solution.py:30
  246.3 4.0 while.4
  250.2 19.7 %custom-call.14 = f32[2,128,128]{1,2,0:T(8,128)S(1)} custom-call(f32[2,128,128]{2,1,0:T(8,128)S(1)} %get-tuple-element.21), custom_call_target="InvertDiagBlocksLowerTriangular" | custom-call | tf_op jit(solution)/shard_map/triangular_solve/custom-call.0 | solution.py:32
  273.0 1.8 copy.37
  275.1 1.9 fusion.6
  279.4 4.4 copy.40
  283.8 116.5 %all-gather.7.cloned.1.call-done = f32[16,256,2,256]{3,1,2,0:T(8,128)} async-done(((f32[1,256,2,256]{3,1,2,0:T(8,128)}), f32[16,256,2,256]{3,1,2,0:T(8,128)}) %all-gather.7.cloned.1.call-update) | async-done | bytes 8388624 | tf_op jit(solution)/shard_map/all_gather | solution.py:26
  400.3 3.7 subtract_select_fusion.1
  405.5 118.6 %reduce-scatter.9.cloned.1.call-done = f32[32,256]{1,0:T(8,128)} async-done(((f32[1024,256]{1,0:T(8,128)}), f32[32,256]{1,0:T(8,128)}) %reduce-scatter.9.cloned.1.call-update) | async-done | bytes 32784 | tf_op jit(solution)/shard_map/reduce_scatter | solution.py:21
  525.8 62.1 %all-gather.9.cloned.1.call-done = f32[1024,256]{1,0:T(8,128)} async-done(((f32[32,256]{1,0:T(8,128)}), f32[1024,256]{1,0:T(8,128)}) %all-gather.9.cloned.1.call-update) | async-done | bytes 1048592 | tf_op jit(solution)/shard_map/all_gather | solution.py:22
  591.6 11.7 %cholesky.164 = f32[128,128]{1,0:T(8,128)S(1)} custom-call(f32[128,128]{1,0:T(8,128)S(1)} %cholesky.197), custom_call_target="Cholesky" | custom-call | tf_op jit(solution)/shard_map/jit(cholesky)/cholesky | solution.py:30
  604.0 9.8 %custom-call.15 = f32[1,128,128]{1,2,0:T(8,128)S(1)} custom-call(f32[1,128,128]{2,1,0:T(8,128)S(1)} %get-tuple-element.48), custom_call_target="InvertDiagBlocksLowerTriangular" | custom-call | tf_op jit(solution)/shard_map/jit(cholesky)/cholesky | solution.py:30
  616.0 11.7 %cholesky.181 = f32[128,128]{1,0:T(8,128)S(1)} custom-call(f32[128,128]{1,0:T(8,128)S(1)} %convolution_subtract_fusion.2), custom_call_target="Cholesky" | custom-call | tf_op jit(solution)/shard_map/jit(cholesky)/cholesky | solution.py:30
  629.6 4.1 while.5
  633.7 19.7 %custom-call.16 = f32[2,128,128]{1,2,0:T(8,128)S(1)} custom-call(f32[2,128,128]{2,1,0:T(8,128)S(1)} %get-tuple-element.22), custom_call_target="InvertDiagBlocksLowerTriangular" | custom-call | tf_op jit(solution)/shard_map/triangular_solve/custom-call.0 | solution.py:32
  657.2 123.3 %all-gather.11.cloned.1.call-done = f32[16,256,2,256]{3,1,2,0:T(8,128)} async-done(((f32[1,256,2,256]{3,1,2,0:T(8,128)}), f32[16,256,2,256]{3,1,2,0:T(8,128)}) %all-gather.11.cloned.1.call-update) | async-done | bytes 8388624 | tf_op jit(solution)/shard_map/all_gather | solution.py:26
  780.5 4.7 fusion
  785.2 6.0 copy.49
  (95 shorter events, 36.2 us)
Async XLA Ops:
  6.5 134.3 %reduce-scatter.7.cloned.1.call-start = ((), (), s32[]{:S(2)}) async-start(), calls=%async_computation.6 | async-start | bytes 1081344 | tf_op jit(solution)/shard_map/reduce_scatter | solution.py:21
  13.8 127.7 %copy-start = (f32[1024,2,1,256]{3,2,1,0:T(1,128)S(1)}, f32[1024,2,1,256]{3,2,1,0:T(1,128)}, u32[]{:S(2)}) copy-start(f32[1024,2,1,256]{3,2,1,0:T(1,128)} %param.5) | copy-start | bytes 6291460
  15.2 189.6 %all-gather.5.cloned.1.call-start = ((), (), s32[]{:S(2)}) async-start(), calls=%async_computation.2 | async-start | bytes 1081344 | tf_op jit(solution)/shard_map/all_gather | solution.py:22
  140.9 259.4 %all-gather.7.cloned.1.call-start = ((), (), s32[]{:S(2)}) async-start(), calls=%async_computation.3 | async-start | bytes 8912896 | tf_op jit(solution)/shard_map/all_gather | solution.py:26
  207.8 0.7 copy-start.3
  277.0 247.1 %reduce-scatter.9.cloned.1.call-start = ((), (), s32[]{:S(2)}) async-start(), calls=%async_computation.7 | async-start | bytes 1081344 | tf_op jit(solution)/shard_map/reduce_scatter | solution.py:21
  279.3 121.0 %copy-start.1 = (f32[1024,256]{1,0:T(8,128)S(1)}, f32[1024,256]{1,0:T(8,128)}, u32[]{:S(2)}) copy-start(f32[1024,256]{1,0:T(8,128)} %all-gather.5.cloned.1.call-done) | copy-start | bytes 3145732
  404.1 121.5 %copy-start.4 = (s32[64]{0:T(128)S(1)}, s32[64]{0:T(128)}, u32[]{:S(2)}) copy-start(s32[64]{0:T(128)} %param.6) | copy-start | bytes 772
  405.5 182.4 %all-gather.9.cloned.1.call-start = ((), (), s32[]{:S(2)}) async-start(), calls=%async_computation.4 | async-start | bytes 1081344 | tf_op jit(solution)/shard_map/all_gather | solution.py:22
  524.1 256.4 %all-gather.11.cloned.1.call-start = ((), (), s32[]{:S(2)}) async-start(), calls=%async_computation.5 | async-start | bytes 8912896 | tf_op jit(solution)/shard_map/all_gather | solution.py:26
  590.9 0.7 copy-start.2
Sparse Core Ops, SparseCore 0:
  15.3 125.5 reduce-scatter.6
  143.0 61.7 all-gather.4
  277.1 123.1 all-gather.6
  405.6 118.4 reduce-scatter.8
  526.1 61.7 all-gather.8
  657.3 123.1 all-gather.10
where the time goes:
time: 809 us; the launch traced here: 799 us
  waiting for transfers between devices  607 us (75%)
  other arithmetic  115 us (14%)
  local copies, waits for them, and re-layouts  35 us (4%)
  between operations  23 us (3%)
  matrix products  17.2 us (2%)
    reduce_scatter x2, waiting for transfers between devices, broadcast_by_parts(): own = lax.psum_scatter(padded, axis, scatter_dimension=0, tiled=True)  244 us
    all_gather x2, waiting for transfers between devices, from_root(): lax.all_gather(array, axis)  240 us
    all_gather x2, waiting for transfers between devices, broadcast_by_parts(): lax.all_gather(own, axis, axis=0, tiled=True)[:len(lines)]  123 us
    another operation x13, other arithmetic, inverse_factor(): lower_factor = jnp.linalg.cholesky(diagonal_block)  68.8 us
    another operation x5, other arithmetic, inverse_factor(): lax.linalg.triangular_solve(lower_factor, identity_block, left_side=True,...  39.4 us
  transfers between devices with their start and end apart: 6, of which 6 were waited for; matrix products, arithmetic and copies ran while one was open for 1% of the time, Pallas kernels for 0%

commit v1 on v0

v1 whole, which is shorter than its diff:
```python
import jax
import jax.numpy as jnp
from jax import lax
from jax.experimental import pallas as pl
from jax.experimental.pallas import tpu as pltpu
from jax.sharding import Mesh, PartitionSpec as P

HI = lax.Precision.HIGHEST
LEAF = 128
PIV = 8


def mm(a, b, ca=1, cb=0, precision=HI):
    return lax.dot_general(
        a, b, (((ca,), (cb,)), ((), ())), precision=precision, preferred_element_type=jnp.float32
    )


def leaf_inverse_factor(matrix):
    tiles = LEAF // 8
    shape = (8, LEAF)
    sub = lax.broadcasted_iota(jnp.int32, shape, 0)
    lane = lax.broadcasted_iota(jnp.int32, shape, 1)
    s = [matrix[8 * t : 8 * t + 8, :] for t in range(tiles)]
    v = [jnp.where(sub + 8 * t == lane, 1.0, 0.0).astype(jnp.float32) for t in range(tiles)]
    scale = [None] * tiles
    for k in range(0, LEAF, PIV):
        t, base = k // 8, k % 8
        piv = {}
        for a in range(PIV):
            for c in range(a + 1):
                piv[a, c] = jnp.broadcast_to(s[t][base + a : base + a + 1, k + c : k + c + 1], shape)
        rd, low = [], {}
        for j in range(PIV):
            rd.append(1.0 / piv[j, j])
            for i in range(j + 1, PIV):
                low[i, j] = piv[i, j] * rd[j]
            for i in range(j + 1, PIV):
                for m in range(j + 1, i + 1):
                    piv[i, m] = piv[i, m] - low[i, j] * piv[m, j]
            root = lax.rsqrt(piv[j, j])
            scale[t] = root if base + j == 0 else jnp.where(sub == base + j, root, scale[t])
        rows_s, rows_v = [], []
        for u in range(t, tiles):
            raw, coef = [], []
            for j in range(PIV):
                c = jnp.broadcast_to(s[u][:, k + j : k + j + 1], shape)
                for m in range(j):
                    c = c - raw[m] * low[j, m]
                raw.append(c)
                c = c * rd[j]
                coef.append(jnp.where(sub > base + j, c, 0.0) if u == t else c)
            for j in range(PIV):
                if u == t:
                    rows_s.append(jnp.broadcast_to(s[t][base + j : base + j + 1, :], shape))
                    rows_v.append(jnp.broadcast_to(v[t][base + j : base + j + 1, :], shape))
                s[u] = s[u] - coef[j] * rows_s[j]
                v[u] = v[u] - coef[j] * rows_v[j]
    return jnp.concatenate([v[t] * scale[t] for t in range(tiles)], axis=0)


def factor_kernel(core_ref, own_ref, other_ref, g_ref, m_ref, h_ref, l_ref):
    n = g_ref.shape[0]
    half = n // 2
    core = core_ref[0]
    for source, part in ((own_ref, core), (other_ref, 1 - core)):
        for c in range(16):
            row = pl.multiple_of(c * 16 + part * 8, 8)
            for i, (top, left) in enumerate(((0, 0), (half, 0), (half, half))):
                for ch in range(2):
                    m_ref[pl.ds(row + top, 8), left + ch * 128 : left + ch * 128 + 128] = source[
                        c % 4, c // 4, i, pl.ds(ch, 8, stride=2), :
                    ]
    h_ref[...] = jnp.zeros_like(h_ref)
    g_ref[...] = jnp.zeros_like(g_ref)
    count = n // LEAF

    def step(k, carry):
        at = pl.multiple_of(k * LEAF, LEAF)
        own = leaf_inverse_factor(m_ref[pl.ds(at, LEAF), pl.ds(at, LEAF)])
        g_ref[pl.ds(at, LEAF), pl.ds(at, LEAF)] = own
        for kk in range(count):

            @pl.when(k == kk)
            def _():
                lo, hi = kk * LEAF, (kk + 1) * LEAF
                if kk:
                    g_ref[lo:hi, 0:lo] = mm(own, h_ref[lo:hi, 0:lo])
                if kk + 1 < count:
                    low = mm(m_ref[hi:n, lo:hi], own, 1, 1)
                    l_ref[hi:n, :] = low
                    for j in range(kk + 1, count):
                        a, b = j * LEAF, (j + 1) * LEAF
                        m_ref[a:n, a:b] = m_ref[a:n, a:b] - mm(l_ref[a:n, :], l_ref[a:b, :], 1, 1)
                    h_ref[hi:n, 0:hi] = h_ref[hi:n, 0:hi] - mm(l_ref[hi:n, :], g_ref[lo:hi, 0:hi])

        return carry

    lax.fori_loop(0, count, step, 0)


def inverse_factor(core, own, other):
    n = 512
    whole = pl.BlockSpec(memory_space=pltpu.VMEM)
    return pl.pallas_call(
        factor_kernel,
        out_shape=jax.ShapeDtypeStruct((n, n), jnp.float32),
        in_specs=[pl.BlockSpec(memory_space=pltpu.SMEM), whole, whole],
        out_specs=whole,
        scratch_shapes=[
            pltpu.VMEM((n, n), jnp.float32),
            pltpu.VMEM((n, n), jnp.float32),
            pltpu.VMEM((n, LEAF), jnp.float32),
        ],
        cost_estimate=pl.CostEstimate(flops=2 * 8 * n**3, bytes_accessed=8 * n * n, transcendentals=n),
    )(core, own, other)


def update_kernel(info_ref, w_ref, own_ref, other_ref, y_ref, g_ref, o_ref, u_ref, z_ref):
    n = g_ref.shape[0]
    step = pl.program_id(0)

    @pl.when(step == 0)
    def _():
        for j in range(4):
            for c in range(16):
                for s in range(2):
                    z_ref[s * 256 + c * 16 : s * 256 + c * 16 + 16, j * 128 : j * 128 + 128] = y_ref[
                        c % 4, c // 4, s, pl.ds(j, 16, stride=4), :
                    ]
        u_ref[...] = mm(g_ref[...], z_ref[...])
        for slot in range(2):
            for s in range(2):

                @pl.when(info_ref[1 + slot] == s)
                def _():
                    rows = lax.broadcasted_iota(jnp.int32, (n, 256), 0)
                    cols = lax.broadcasted_iota(jnp.int32, (n, 256), 1)
                    u_ref[:, slot * 256 : slot * 256 + 256] = jnp.where(
                        rows == cols + s * 256, 1.0, 0.0
                    ).astype(jnp.float32)

        solved = mm(g_ref[...], u_ref[...], 0, 0)
        at = 0
        for yh in range(4):
            for zlo in range(2):
                for half in range(2):
                    for s in range(2):
                        row = s * 256 + (half * 8 + zlo * 4 + yh) * 16
                        z_ref[at : at + 16, :] = solved[row : row + 16, :]
                        at += 16

    def rows_of(source, yl):
        for ch in range(2):
            panel = jnp.concatenate(
                [source[yh, yl, pl.ds(ch, 128, stride=2), :] for yh in range(4)], axis=0
            )
            change = mm(panel, z_ref[...], 0, 0)
            for j in range(4):
                hit = info_ref[1 + j // 2] >= 0
                keep = jnp.where(hit, 0.0, 1.0).astype(jnp.float32)
                sign = jnp.where(hit, 1.0, -1.0).astype(jnp.float32)
                at = pl.ds(ch * 512 + j, 128, stride=4)
                o_ref[at, :] = keep * w_ref[at, :] + sign * change[:, j * 128 : j * 128 + 128]

    for o, source in enumerate((own_ref, other_ref)):
        for yl in range(2):

            @pl.when(step == o * 2 + yl)
            def _():
                rows_of(source, yl)


def update(info, working, own, other, across, factor):
    n = 512
    whole = pl.BlockSpec(memory_space=pltpu.VMEM)

    def block(step, info_ref):
        core = info_ref[0]
        part = jnp.where(step >= 2, 1 - core, core)
        return (step % 2) * 2 + part, 0

    return pl.pallas_call(
        update_kernel,
        out_shape=jax.ShapeDtypeStruct(working.shape, jnp.float32),
        grid_spec=pltpu.PrefetchScalarGridSpec(
            num_scalar_prefetch=1,
            grid=(4,),
            in_specs=[pl.BlockSpec((1024, 128), block), whole, whole, whole, whole],
            out_specs=pl.BlockSpec((1024, 128), block),
            scratch_shapes=[pltpu.VMEM((n, n), jnp.float32), pltpu.VMEM((n, n), jnp.float32)],
        ),
        cost_estimate=pl.CostEstimate(flops=8 * n**3, bytes_accessed=8 * 2**20, transcendentals=0),
    )(info, working, own, other, across, factor)


def swap(array, axis):
    return lax.ppermute(array, axis, [(0, 1), (1, 0)])


def ordered_pair(own, other, index):
    first = jnp.where(index == 0, own, other)
    second = jnp.where(index == 0, other, own)
    return jnp.stack([first, second])


def spread_pairs(swapped):
    pairs = []
    for source in range(512):
        blk, row = divmod(source, 16)
        upper = (row >= 8) != swapped
        target_row = blk // 4 + (8 if upper else 0)
        target_blk = (row % 8) * 4 + blk % 4
        pairs.append((source, target_blk * 16 + target_row))
    return pairs


EVERY = ("zlo", "y", "core", "x", "zhi")
ROWS = ("x", "zhi")


def pick(array, axis, index):
    return lax.dynamic_index_in_dim(array, index, axis, keepdims=False)


def exchange(array, axis):
    return lax.all_to_all(array, axis, 0, 0, tiled=True)


def copies(array, count):
    return jnp.broadcast_to(array, (count, *array.shape))


def doubled(array, axis):
    index = lax.axis_index(axis)
    near = lax.ppermute(array, axis, [(i, i ^ 1) for i in range(4)])
    pair = ordered_pair(array, near, index % 2)
    far = lax.ppermute(pair, axis, [(i, i ^ 2) for i in range(4)])
    return ordered_pair(pair, far, index // 2).reshape(4, *array.shape)


def local(covariance, panel_order):
    row = lax.axis_index(ROWS)
    core = lax.axis_index("core")
    zlo = lax.axis_index("zlo")
    blk = lax.axis_index(("zlo", "y", "core"))
    working = covariance.reshape(4096, 128)
    target = [panel_order[0], panel_order[1]]
    root = [q // 4 for q in target]
    owner = [q % 32 for q in target]
    slot = [q // 32 for q in target]

    cand = [lax.dynamic_slice_in_dim(working, (q % 4) * 1024, 1024, 0).reshape(4, 4, 64, 128) for q in target]
    got = exchange(jnp.stack(cand, axis=2), "x")
    got = jnp.stack([pick(got[:, :, s], 0, root[s] // 4) for s in range(2)], axis=1)
    got = exchange(got, "zhi")
    chunk = jnp.stack([pick(got[:, s], 0, root[s] % 4) for s in range(2)])
    by_slot = chunk.reshape(2, 16, 2, 2, 128)

    part = [pick(by_slot[1 if i else 0], 1, slot[1 if i == 2 else 0]) for i in range(3)]
    blocks = jnp.stack(part).reshape(3, 2, 16, 128)
    source = jnp.stack([owner[0], owner[0], owner[1]])
    other = swap(pick(blocks, 1, 1 - core), "core")
    mine = jnp.where((source % 2 == core)[:, None, None], pick(blocks, 1, core), other)
    mine = jnp.where((source // 16 == zlo)[:, None, None], mine, swap(mine, "zlo"))
    spread = exchange(copies(mine, 8), "y")
    from_y = source // 2 % 8
    mine = jnp.stack([pick(spread[:, i], 0, from_y[i]) for i in range(3)])
    ready = mine
    mine = doubled(doubled(mine, "x"), "zhi")
    factor = inverse_factor(core.reshape(1), mine, swap(mine, "core"))

    low, high = by_slot[:, :, 0].reshape(64, 128), by_slot[:, :, 1].reshape(64, 128)
    upper = row >= 8
    piece_a = lax.ppermute(jnp.where(upper, high, low), EVERY, spread_pairs(False))
    piece_b = lax.ppermute(jnp.where(upper, low, high), EVERY, spread_pairs(True))
    pieces = jnp.stack([jnp.where(upper, piece_b, piece_a), jnp.where(upper, piece_a, piece_b)])
    pieces = ordered_pair(pieces, swap(pieces, "zlo"), zlo).reshape(256, 128)
    pieces = lax.optimization_barrier((pieces, ready))[0]
    pieces = exchange(copies(pieces, 8), "y").reshape(4, 2, 256, 128)

    across = lax.optimization_barrier((doubled(chunk, "x"), pieces))[0]
    across = exchange(copies(across, 4), "zhi")

    hits = [jnp.int32(-1), jnp.int32(-1)]
    for i in range(2):
        for s in range(2):
            hits[i] = jnp.where(target[s] == i * 32 + blk, s, hits[i])
    info = jnp.stack([core, hits[0], hits[1]]).astype(jnp.int32)
    result = update(info, working, pieces, swap(pieces, "core"), across, factor)
    return result.reshape(1024, 2, 1, 256)


def solution(mesh):
    fine = Mesh(mesh.devices.reshape(2, 8, 2, 4, 4), EVERY)
    spec = P(ROWS, None, ("zlo", "y", "core"), None)
    return jax.shard_map(local, mesh=fine, in_specs=(spec, P()), out_specs=spec, check_vma=False)
```

time: 809 us -> 207 us (0.26)
  the two profiles are of different devices: /device:TPU:2 before, /device:TPU:65 now
where the time goes in v1:
time: 207 us; the launch traced here: 206 us
  starting transfers between devices  86.6 us (42%)
  waiting for transfers between devices  59.3 us (29%)
  Pallas kernels  34.2 us (17%)
  between operations  13.8 us (7%)
  local copies, waits for them, and re-layouts  8.48 us (4%)
  other arithmetic  3.87 us (2%)
    all_to_all x5, starting transfers between devices, exchange(): return lax.all_to_all(array, axis, 0, 0, tiled=True)  40.7 us
    all_to_all x5, waiting for transfers between devices, exchange(): return lax.all_to_all(array, axis, 0, 0, tiled=True)  29.6 us
    ppermute x3, waiting for transfers between devices, doubled(): far = lax.ppermute(pair, axis, [(i, i ^ 2) for i in range(4)])  25.3 us
    pallas_call x1, Pallas kernels, inverse_factor(): pl.pallas_call(factor_kernel, out_shape=jax.ShapeDtypeStruct((n, n), jnp....  21.6 us
    ppermute x5, starting transfers between devices, swap(): return lax.ppermute(array, axis, [(0, 1), (1, 0)])  19.5 us
    ppermute x3, starting transfers between devices, doubled(): far = lax.ppermute(pair, axis, [(i, i ^ 2) for i in range(4)])  14.1 us
    pallas_call x1, Pallas kernels, update(): pl.pallas_call(update_kernel, out_shape=jax.ShapeDtypeStruct(working.shap...  12.6 us
    ppermute x3, starting transfers between devices, doubled(): near = lax.ppermute(array, axis, [(i, i ^ 1) for i in range(4)])  7.08 us
  transfers between devices with their start and end apart: 18, of which 9 were waited for; matrix products, arithmetic and copies ran while one was open for 2% of the time, Pallas kernels for 10%

profile of v1, /device:TPU:65, one launch (start us, length us, event | category | flops | bytes accessed | tf_op | source)
XLA Modules:
  0.0 206.2 jit_solution(17577693029311820083)
XLA Ops:
  7.5 4.0 %all-to-all-start = ((f32[4,4,2,64,128]{4,3,1,2,0:T(8,128)}), f32[4,4,2,64,128]{4,3,1,2,0:T(8,128)S(1)}, u32[]{:S(2)}, u32[]{:S(2)}) async-start(f32[4,4,2,64,128]{4,3,1,2,0:T(8,128)} %pad_maximum_fusion), calls=%async_computation | async-start | bytes 2097152 | tf_op jit(solution)/shard_map/all_to_all | solution.py:227
  12.9 12.9 %all-to-all-done = f32[4,4,2,64,128]{4,3,1,2,0:T(8,128)S(1)} async-done(((f32[4,4,2,64,128]{4,3,1,2,0:T(8,128)}), f32[4,4,2,64,128]{4,3,1,2,0:T(8,128)S(1)}, u32[]{:S(2)}, u32[]{:S(2)}) %all-to-all-start) | async-done | bytes 1048608 | tf_op jit(solution)/shard_map/all_to_all | solution.py:227
  26.6 9.1 %all-to-all-start.1 = ((f32[4,2,64,128]{3,2,1,0:T(8,128)}), f32[4,2,64,128]{3,2,1,0:T(8,128)S(1)}, u32[]{:S(2)}, u32[]{:S(2)}) async-start(f32[4,2,64,128]{3,2,1,0:T(8,128)} %pad_maximum_fusion.2), calls=%async_computation.1 | async-start | bytes 524288 | tf_op jit(solution)/shard_map/all_to_all | solution.py:227
  43.9 6.1 %collective-permute-start.3 = (f32[3,16,128]{2,1,0:T(8,128)S(1)}, f32[3,16,128]{2,1,0:T(8,128)S(1)}, u32[]{:S(2)}, u32[]{:S(2)}) collective-permute-start(f32[3,16,128]{2,1,0:T(8,128)S(1)} %dynamic-slice_bitcast_fusion.2), channel_id=1, source_target_pairs={{0,16},{16,0},{1,17},{17,1},{2,18},{18,2},{3,19},{19,3},{4,20},{20... | collective-permute-start | bytes 73736 | tf_op jit(solution)/shard_map/ppermute | solution.py:198
  50.1 1.9 collective-permute-start.1
  52.0 3.4 %collective-permute-start = (f32[64,128]{1,0:T(8,128)S(1)}, f32[64,128]{1,0:T(8,128)S(1)}, u32[]{:S(2)}, u32[]{:S(2)}) collective-permute-start(f32[64,128]{1,0:T(8,128)S(1)} %bitcast.98), channel_id=1, source_target_pairs={{0,8},{1,72},{2,136},{3,200},{4,264},{5,328},{6,392},{7,456},{8,0}... | collective-permute-start | bytes 98312 | tf_op jit(solution)/shard_map/ppermute | solution.py:276
  58.8 2.1 collective-permute-start.2
  61.6 17.9 %all-to-all-start.2 = ((f32[8,3,16,128]{3,2,1,0:T(8,128)}), f32[8,3,16,128]{3,2,1,0:T(8,128)S(1)}, u32[]{:S(2)}, u32[]{:S(2)}) async-start(f32[8,3,16,128]{3,2,1,0:T(8,128)} %broadcast_in_dim.26), calls=%async_computation.2 | async-start | bytes 393216 | tf_op jit(solution)/shard_map/all_to_all | solution.py:227
  79.5 8.5 %all-to-all-done.2 = f32[8,3,16,128]{3,2,1,0:T(8,128)S(1)} async-done(((f32[8,3,16,128]{3,2,1,0:T(8,128)}), f32[8,3,16,128]{3,2,1,0:T(8,128)S(1)}, u32[]{:S(2)}, u32[]{:S(2)}) %all-to-all-start.2) | async-done | bytes 196640 | tf_op jit(solution)/shard_map/all_to_all | solution.py:227
  89.2 3.6 %all-to-all-start.3 = ((f32[8,256,128]{2,1,0:T(8,128)}), f32[8,256,128]{2,1,0:T(8,128)S(1)}, u32[]{:S(2)}, u32[]{:S(2)}) async-start(f32[8,256,128]{2,1,0:T(8,128)} %broadcast_in_dim.27), calls=%async_computation.3 | async-start | bytes 2097152 | tf_op jit(solution)/shard_map/all_to_all | solution.py:227
  92.8 1.9 collective-permute-start.6
  94.8 3.1 %collective-permute-done.6 = f32[2,64,128]{2,1,0:T(8,128)S(1)} collective-permute-done((f32[2,64,128]{2,1,0:T(8,128)S(1)}, f32[2,64,128]{2,1,0:T(8,128)S(1)}, u32[]{:S(2)}, u32[]{:S(2)}) %collective-permute-start.6) | collective-permute-done | bytes 65568 | tf_op jit(solution)/shard_map/ppermute | solution.py:236
  99.8 3.4 %collective-permute-start.7 = (f32[2,2,64,128]{3,2,1,0:T(8,128)S(1)}, f32[2,2,64,128]{3,2,1,0:T(8,128)S(1)}, u32[]{:S(2)}, u32[]{:S(2)}) collective-permute-start(f32[2,2,64,128]{3,2,1,0:T(8,128)S(1)} %pad_maximum_fusion.6), channel_id=1, source_target_pairs={{0,8},{4,12},{8,0},{12,4},{1,9},{5,13},{9,1},{13,5},{2,10},{6,14},... | collective-permute-start | bytes 393224 | tf_op jit(solution)/shard_map/ppermute | solution.py:238
  103.3 3.4 %collective-permute-start.9 = (f32[2,3,16,128]{3,2,1,0:T(8,128)S(1)}, f32[2,3,16,128]{3,2,1,0:T(8,128)S(1)}, u32[]{:S(2)}, u32[]{:S(2)}) collective-permute-start(f32[2,3,16,128]{3,2,1,0:T(8,128)S(1)} %pad_maximum_fusion.11), channel_id=1, source_target_pairs={{0,8},{4,12},{8,0},{12,4},{1,9},{5,13},{9,1},{13,5},{2,10},{6,14},... | collective-permute-start | bytes 147464 | tf_op jit(solution)/shard_map/ppermute | solution.py:238
  107.6 2.3 %collective-permute-done.9 = f32[2,3,16,128]{3,2,1,0:T(8,128)S(1)} collective-permute-done((f32[2,3,16,128]{3,2,1,0:T(8,128)S(1)}, f32[2,3,16,128]{3,2,1,0:T(8,128)S(1)}, u32[]{:S(2)}, u32[]{:S(2)}) %collective-permute-start.9) | collective-permute-done | bytes 49184 | tf_op jit(solution)/shard_map/ppermute | solution.py:238
  109.9 3.2 %collective-permute-start.10 = (f32[4,3,16,128]{3,2,1,0:T(8,128)S(1)}, f32[4,3,16,128]{3,2,1,0:T(8,128)S(1)}, u32[]{:S(2)}, u32[]{:S(2)}) collective-permute-start(f32[4,3,16,128]{3,2,1,0:T(8,128)S(1)} %bitcast.90), channel_id=1, source_target_pairs={{0,1},{1,0},{2,3},{3,2},{4,5},{5,4},{6,7},{7,6},{8,9},{9,8},{10,11... | collective-permute-start | bytes 294920 | tf_op jit(solution)/shard_map/ppermute | solution.py:236
  113.2 6.6 %all-to-all-done.3 = f32[8,256,128]{2,1,0:T(8,128)S(1)} async-done(((f32[8,256,128]{2,1,0:T(8,128)}), f32[8,256,128]{2,1,0:T(8,128)S(1)}, u32[]{:S(2)}, u32[]{:S(2)}) %all-to-all-start.3) | async-done | bytes 1048608 | tf_op jit(solution)/shard_map/all_to_all | solution.py:227
  121.0 6.1 %all-to-all-start.4 = ((f32[4,4,2,64,128]{4,3,2,1,0:T(8,128)}), f32[4,4,2,64,128]{4,3,2,1,0:T(8,128)S(1)}, u32[]{:S(2)}, u32[]{:S(2)}) async-start(f32[4,4,2,64,128]{4,3,2,1,0:T(8,128)} %broadcast_in_dim.28), calls=%async_computation.4 | async-start | bytes 2097152 | tf_op jit(solution)/shard_map/all_to_all | solution.py:227
  127.2 7.3 %collective-permute-start.11 = (f32[2,4,3,16,128]{4,3,2,1,0:T(8,128)S(1)}, f32[2,4,3,16,128]{4,3,2,1,0:T(8,128)}, u32[]{:S(2)}, u32[]{:S(2)}) collective-permute-start(f32[2,4,3,16,128]{4,3,2,1,0:T(8,128)S(1)} %pad_maximum_fusion.4), channel_id=1, source_target_pairs={{0,2},{1,3},{2,0},{3,1},{4,6},{5,7},{6,4},{7,5},{8,10},{9,11},{10,... | collective-permute-start | bytes 589832 | tf_op jit(solution)/shard_map/ppermute | solution.py:238
  134.5 5.3 %collective-permute-start.5 = (f32[4,2,256,128]{3,2,1,0:T(8,128)S(1)}, f32[4,2,256,128]{3,2,1,0:T(8,128)S(1)}, u32[]{:S(2)}, u32[]{:S(2)}) collective-permute-start(f32[4,2,256,128]{3,2,1,0:T(8,128)S(1)} %bitcast.82), channel_id=1, source_target_pairs={{0,16},{16,0},{1,17},{17,1},{2,18},{18,2},{3,19},{19,3},{4,20},{20... | collective-permute-start | bytes 3145736 | tf_op jit(solution)/shard_map/ppermute | solution.py:198
  139.9 22.0 %collective-permute-done.11 = f32[2,4,3,16,128]{4,3,2,1,0:T(8,128)} collective-permute-done((f32[2,4,3,16,128]{4,3,2,1,0:T(8,128)S(1)}, f32[2,4,3,16,128]{4,3,2,1,0:T(8,128)}, u32[]{:S(2)}, u32[]{:S(2)}) %collective-permute-start.11) | collective-permute-done | bytes 196640 | tf_op jit(solution)/shard_map/ppermute | solution.py:238
  162.9 4.1 %collective-permute-start.12 = (f32[4,4,3,16,128]{4,3,2,1,0:T(8,128)S(1)}, f32[4,4,3,16,128]{4,3,2,1,0:T(8,128)}, u32[]{:S(2)}, u32[]{:S(2)}) collective-permute-start(f32[4,4,3,16,128]{4,3,2,1,0:T(8,128)S(1)} %bitcast.88), channel_id=1, source_target_pairs={{0,16},{16,0},{1,17},{17,1},{2,18},{18,2},{3,19},{19,3},{4,20},{20... | collective-permute-start | bytes 1179656 | tf_op jit(solution)/shard_map/ppermute | solution.py:198
  170.1 21.6 %shard_map.28.g_ref = f32[512,512]{1,0:T(8,128)} custom-call(s32[1]{0:T(128)} %bitcast.core_ref, f32[4,4,3,16,128]{4,3,2,1,0:T(8,128)} %bitcast.89, f32[4,4,3,16,128]{4,3,2,1,0:T(8,128)} %collective-permute-done.12.other_ref), custom_call_target="tpu_custom_call" | custom-call | flops 2147483648 | bytes 2097152 | tf_op jit(solution)/shard_map/pallas_call | solution.py:105
  193.6 12.6 %shard_map.29 = f32[4096,128]{1,0:T(8,128)} custom-call(s32[3]{0:T(128)} %pad_add_fusion.info_ref, f32[4096,128]{1,0:T(8,128)} %bitcast.81, f32[4,2,256,128]{3,2,1,0:T(8,128)} %bitcast.83, f32[4,2,256,128]{3,2,1,0:T(8,128)} %copy-done.2, f32[4,4,2,64,128]{4,3,2,1,0:T(8,128)} %copy-done.1, f32[512,512]{1,0:T(8,128)} %shard_map.28.g_ref), custom_call_target="tpu_custom_call" | custom-call | flops 1073741824 | bytes 8388608 | tf_op jit(solution)/shard_map/pallas_call | solution.py:183
  (69 shorter events, 20.1 us)
Async XLA Ops:
  7.5 18.3 %all-to-all-start = ((f32[4,4,2,64,128]{4,3,1,2,0:T(8,128)}), f32[4,4,2,64,128]{4,3,1,2,0:T(8,128)S(1)}, u32[]{:S(2)}, u32[]{:S(2)}) async-start(f32[4,4,2,64,128]{4,3,1,2,0:T(8,128)} %pad_maximum_fusion), calls=%async_computation | async-start | bytes 2097152 | tf_op jit(solution)/shard_map/all_to_all | solution.py:227
  26.6 17.2 %all-to-all-start.1 = ((f32[4,2,64,128]{3,2,1,0:T(8,128)}), f32[4,2,64,128]{3,2,1,0:T(8,128)S(1)}, u32[]{:S(2)}, u32[]{:S(2)}) async-start(f32[4,2,64,128]{3,2,1,0:T(8,128)} %pad_maximum_fusion.2), calls=%async_computation.1 | async-start | bytes 524288 | tf_op jit(solution)/shard_map/all_to_all | solution.py:227
  43.9 11.5 %collective-permute-start.3 = (f32[3,16,128]{2,1,0:T(8,128)S(1)}, f32[3,16,128]{2,1,0:T(8,128)S(1)}, u32[]{:S(2)}, u32[]{:S(2)}) collective-permute-start(f32[3,16,128]{2,1,0:T(8,128)S(1)} %dynamic-slice_bitcast_fusion.2), channel_id=1, source_target_pairs={{0,16},{16,0},{1,17},{17,1},{2,18},{18,2},{3,19},{19,3},{4,20},{20... | collective-permute-start | bytes 73736 | tf_op jit(solution)/shard_map/ppermute | solution.py:198
  50.1 7.4 %collective-permute-start.1 = (f32[64,128]{1,0:T(8,128)S(1)}, f32[64,128]{1,0:T(8,128)S(1)}, u32[]{:S(2)}, u32[]{:S(2)}) collective-permute-start(f32[64,128]{1,0:T(8,128)S(1)} %bitcast.99), channel_id=1, source_target_pairs={{0,0},{1,64},{2,128},{3,192},{4,256},{5,320},{6,384},{7,448},{8,8}... | collective-permute-start | bytes 98312 | tf_op jit(solution)/shard_map/ppermute | solution.py:275
  52.0 6.8 %collective-permute-start = (f32[64,128]{1,0:T(8,128)S(1)}, f32[64,128]{1,0:T(8,128)S(1)}, u32[]{:S(2)}, u32[]{:S(2)}) collective-permute-start(f32[64,128]{1,0:T(8,128)S(1)} %bitcast.98), channel_id=1, source_target_pairs={{0,8},{1,72},{2,136},{3,200},{4,264},{5,328},{6,392},{7,456},{8,0}... | collective-permute-start | bytes 98312 | tf_op jit(solution)/shard_map/ppermute | solution.py:276
  55.5 5.3 %collective-permute-start.4 = (f32[3,16,128]{2,1,0:T(8,128)S(1)}, f32[3,16,128]{2,1,0:T(8,128)S(1)}, u32[]{:S(2)}, u32[]{:S(2)}) collective-permute-start(f32[3,16,128]{2,1,0:T(8,128)S(1)} %bitcast_select_fusion), channel_id=1, source_target_pairs={{0,256},{256,0},{1,257},{257,1},{2,258},{258,2},{3,259},{259,3},{4... | collective-permute-start | bytes 73736 | tf_op jit(solution)/shard_map/ppermute | solution.py:198
  58.8 20.7 %collective-permute-start.2 = (f32[2,64,128]{2,1,0:T(8,128)S(1)}, f32[2,64,128]{2,1,0:T(8,128)S(1)}, u32[]{:S(2)}, u32[]{:S(2)}) collective-permute-start(f32[2,64,128]{2,1,0:T(8,128)S(1)} %pad_maximum_fusion.8), channel_id=1, source_target_pairs={{0,256},{256,0},{1,257},{257,1},{2,258},{258,2},{3,259},{259,3},{4... | collective-permute-start | bytes 196616 | tf_op jit(solution)/shard_map/ppermute | solution.py:198
  61.6 26.4 %all-to-all-start.2 = ((f32[8,3,16,128]{3,2,1,0:T(8,128)}), f32[8,3,16,128]{3,2,1,0:T(8,128)S(1)}, u32[]{:S(2)}, u32[]{:S(2)}) async-start(f32[8,3,16,128]{3,2,1,0:T(8,128)} %broadcast_in_dim.26), calls=%async_computation.2 | async-start | bytes 393216 | tf_op jit(solution)/shard_map/all_to_all | solution.py:227
  89.2 30.6 %all-to-all-start.3 = ((f32[8,256,128]{2,1,0:T(8,128)}), f32[8,256,128]{2,1,0:T(8,128)S(1)}, u32[]{:S(2)}, u32[]{:S(2)}) async-start(f32[8,256,128]{2,1,0:T(8,128)} %broadcast_in_dim.27), calls=%async_computation.3 | async-start | bytes 2097152 | tf_op jit(solution)/shard_map/all_to_all | solution.py:227
  92.8 5.0 %collective-permute-start.6 = (f32[2,64,128]{2,1,0:T(8,128)S(1)}, f32[2,64,128]{2,1,0:T(8,128)S(1)}, u32[]{:S(2)}, u32[]{:S(2)}) collective-permute-start(f32[2,64,128]{2,1,0:T(8,128)S(1)} %pad_maximum_fusion.9), channel_id=1, source_target_pairs={{0,4},{4,0},{8,12},{12,8},{1,5},{5,1},{9,13},{13,9},{2,6},{6,2},{1... | collective-permute-start | bytes 196616 | tf_op jit(solution)/shard_map/ppermute | solution.py:236
  97.8 5.4 %collective-permute-start.8 = (f32[3,16,128]{2,1,0:T(8,128)S(1)}, f32[3,16,128]{2,1,0:T(8,128)S(1)}, u32[]{:S(2)}, u32[]{:S(2)}) collective-permute-start(f32[3,16,128]{2,1,0:T(8,128)S(1)} %pad_maximum_fusion.13), channel_id=1, source_target_pairs={{0,4},{4,0},{8,12},{12,8},{1,5},{5,1},{9,13},{13,9},{2,6},{6,2},{1... | collective-permute-start | bytes 73736 | tf_op jit(solution)/shard_map/ppermute | solution.py:236
  99.8 7.8 %collective-permute-start.7 = (f32[2,2,64,128]{3,2,1,0:T(8,128)S(1)}, f32[2,2,64,128]{3,2,1,0:T(8,128)S(1)}, u32[]{:S(2)}, u32[]{:S(2)}) collective-permute-start(f32[2,2,64,128]{3,2,1,0:T(8,128)S(1)} %pad_maximum_fusion.6), channel_id=1, source_target_pairs={{0,8},{4,12},{8,0},{12,4},{1,9},{5,13},{9,1},{13,5},{2,10},{6,14},... | collective-permute-start | bytes 393224 | tf_op jit(solution)/shard_map/ppermute | solution.py:238
  103.3 6.6 %collective-permute-start.9 = (f32[2,3,16,128]{3,2,1,0:T(8,128)S(1)}, f32[2,3,16,128]{3,2,1,0:T(8,128)S(1)}, u32[]{:S(2)}, u32[]{:S(2)}) collective-permute-start(f32[2,3,16,128]{3,2,1,0:T(8,128)S(1)} %pad_maximum_fusion.11), channel_id=1, source_target_pairs={{0,8},{4,12},{8,0},{12,4},{1,9},{5,13},{9,1},{13,5},{2,10},{6,14},... | collective-permute-start | bytes 147464 | tf_op jit(solution)/shard_map/ppermute | solution.py:238
  109.9 17.2 %collective-permute-start.10 = (f32[4,3,16,128]{3,2,1,0:T(8,128)S(1)}, f32[4,3,16,128]{3,2,1,0:T(8,128)S(1)}, u32[]{:S(2)}, u32[]{:S(2)}) collective-permute-start(f32[4,3,16,128]{3,2,1,0:T(8,128)S(1)} %bitcast.90), channel_id=1, source_target_pairs={{0,1},{1,0},{2,3},{3,2},{4,5},{5,4},{6,7},{7,6},{8,9},{9,8},{10,11... | collective-permute-start | bytes 294920 | tf_op jit(solution)/shard_map/ppermute | solution.py:236
  119.8 14.7 %copy-start = (f32[8,256,128]{2,1,0:T(8,128)}, f32[8,256,128]{2,1,0:T(8,128)S(1)}, u32[]{:S(2)}) copy-start(f32[8,256,128]{2,1,0:T(8,128)S(1)} %all-to-all-done.3) | copy-start | bytes 3145732
  121.0 70.6 %all-to-all-start.4 = ((f32[4,4,2,64,128]{4,3,2,1,0:T(8,128)}), f32[4,4,2,64,128]{4,3,2,1,0:T(8,128)S(1)}, u32[]{:S(2)}, u32[]{:S(2)}) async-start(f32[4,4,2,64,128]{4,3,2,1,0:T(8,128)} %broadcast_in_dim.28), calls=%async_computation.4 | async-start | bytes 2097152 | tf_op jit(solution)/shard_map/all_to_all | solution.py:227
  127.2 34.7 %collective-permute-start.11 = (f32[2,4,3,16,128]{4,3,2,1,0:T(8,128)S(1)}, f32[2,4,3,16,128]{4,3,2,1,0:T(8,128)}, u32[]{:S(2)}, u32[]{:S(2)}) collective-permute-start(f32[2,4,3,16,128]{4,3,2,1,0:T(8,128)S(1)} %pad_maximum_fusion.4), channel_id=1, source_target_pairs={{0,2},{1,3},{2,0},{3,1},{4,6},{5,7},{6,4},{7,5},{8,10},{9,11},{10,... | collective-permute-start | bytes 589832 | tf_op jit(solution)/shard_map/ppermute | solution.py:238
  134.5 57.2 %collective-permute-start.5 = (f32[4,2,256,128]{3,2,1,0:T(8,128)S(1)}, f32[4,2,256,128]{3,2,1,0:T(8,128)S(1)}, u32[]{:S(2)}, u32[]{:S(2)}) collective-permute-start(f32[4,2,256,128]{3,2,1,0:T(8,128)S(1)} %bitcast.82), channel_id=1, source_target_pairs={{0,16},{16,0},{1,17},{17,1},{2,18},{18,2},{3,19},{19,3},{4,20},{20... | collective-permute-start | bytes 3145736 | tf_op jit(solution)/shard_map/ppermute | solution.py:198
  162.9 7.2 %copy-start.3 = (f32[2,2,4,3,16,128]{5,4,3,2,1,0:T(8,128)}, f32[2,2,4,3,16,128]{5,4,3,2,1,0:T(8,128)S(1)}, u32[]{:S(2)}) copy-start(f32[2,2,4,3,16,128]{5,4,3,2,1,0:T(8,128)S(1)} %pad_maximum_fusion.1) | copy-start | bytes 1179652
  162.9 7.2 %collective-permute-start.12 = (f32[4,4,3,16,128]{4,3,2,1,0:T(8,128)S(1)}, f32[4,4,3,16,128]{4,3,2,1,0:T(8,128)}, u32[]{:S(2)}, u32[]{:S(2)}) collective-permute-start(f32[4,4,3,16,128]{4,3,2,1,0:T(8,128)S(1)} %bitcast.88), channel_id=1, source_target_pairs={{0,16},{16,0},{1,17},{17,1},{2,18},{18,2},{3,19},{19,3},{4,20},{20... | collective-permute-start | bytes 1179656 | tf_op jit(solution)/shard_map/ppermute | solution.py:198
  191.7 1.0 copy-start.2
  192.7 1.0 copy-start.1

commit v2 on v1

--- a/solution.py
+++ b/solution.py
@@ -4,6 +4,7 @@
 from jax.experimental import pallas as pl
 from jax.experimental.pallas import tpu as pltpu
 from jax.sharding import Mesh, PartitionSpec as P
+
 
 HI = lax.Precision.HIGHEST
 LEAF = 128
@@ -69,7 +70,7 @@
             for i, (top, left) in enumerate(((0, 0), (half, 0), (half, half))):
                 for ch in range(2):
                     m_ref[pl.ds(row + top, 8), left + ch * 128 : left + ch * 128 + 128] = source[
-                        c % 4, c // 4, i, pl.ds(ch, 8, stride=2), :
+                        c // 4, c % 4, i, pl.ds(ch, 8, stride=2), :
                     ]
     h_ref[...] = jnp.zeros_like(h_ref)
     g_ref[...] = jnp.zeros_like(g_ref)
@@ -126,7 +127,7 @@
             for c in range(16):
                 for s in range(2):
                     z_ref[s * 256 + c * 16 : s * 256 + c * 16 + 16, j * 128 : j * 128 + 128] = y_ref[
-                        c % 4, c // 4, s, pl.ds(j, 16, stride=4), :
+                        c // 4, c % 4, s, pl.ds(j, 16, stride=4), :
                     ]
         u_ref[...] = mm(g_ref[...], z_ref[...])
         for slot in range(2):
@@ -239,59 +240,71 @@
     return ordered_pair(pair, far, index // 2).reshape(4, *array.shape)
 
 
-def local(covariance, panel_order):
-    row = lax.axis_index(ROWS)
-    core = lax.axis_index("core")
-    zlo = lax.axis_index("zlo")
-    blk = lax.axis_index(("zlo", "y", "core"))
+def after(array, *others):
+    return lax.optimization_barrier((array, *others))[0]
+
+
+def sections(covariance, panel_order):
+    place = lax.axis_index(EVERY)
+    row, core, zlo, blk = place & 15, (place >> 4) & 1, place >> 8, place >> 4
     working = covariance.reshape(4096, 128)
     target = [panel_order[0], panel_order[1]]
-    root = [q // 4 for q in target]
-    owner = [q % 32 for q in target]
-    slot = [q // 32 for q in target]
-
-    cand = [lax.dynamic_slice_in_dim(working, (q % 4) * 1024, 1024, 0).reshape(4, 4, 64, 128) for q in target]
+    root = [q >> 2 for q in target]
+
+    cand = [lax.dynamic_slice_in_dim(working, (q & 3) << 10, 1024, 0).reshape(4, 4, 64, 128) for q in target]
     got = exchange(jnp.stack(cand, axis=2), "x")
-    got = jnp.stack([pick(got[:, :, s], 0, root[s] // 4) for s in range(2)], axis=1)
+    got = jnp.stack([pick(got[:, :, s], 0, root[s] >> 2) for s in range(2)], axis=1)
     got = exchange(got, "zhi")
-    chunk = jnp.stack([pick(got[:, s], 0, root[s] % 4) for s in range(2)])
+    chunk = jnp.stack([pick(got[:, s], 0, root[s] & 3) for s in range(2)])
     by_slot = chunk.reshape(2, 16, 2, 2, 128)
 
-    part = [pick(by_slot[1 if i else 0], 1, slot[1 if i == 2 else 0]) for i in range(3)]
+    part = [pick(by_slot[1 if i else 0], 1, target[1 if i == 2 else 0] >> 5) for i in range(3)]
     blocks = jnp.stack(part).reshape(3, 2, 16, 128)
-    source = jnp.stack([owner[0], owner[0], owner[1]])
+    source = [target[0], target[0], target[1]]
+
+    def chosen(shift, index, own, other):
+        return jnp.stack([jnp.where(((source[i] >> shift) & 1) == index, own[i], other[i]) for i in range(3)])
+
     other = swap(pick(blocks, 1, 1 - core), "core")
-    mine = jnp.where((source % 2 == core)[:, None, None], pick(blocks, 1, core), other)
-    mine = jnp.where((source // 16 == zlo)[:, None, None], mine, swap(mine, "zlo"))
+    mine = chosen(0, core, pick(blocks, 1, core), other)
+    other = swap(mine, "zlo")
+    placed = mine = chosen(4, zlo, mine, other)
     spread = exchange(copies(mine, 8), "y")
-    from_y = source // 2 % 8
-    mine = jnp.stack([pick(spread[:, i], 0, from_y[i]) for i in range(3)])
+    mine = jnp.stack([pick(spread[:, i], 0, (source[i] >> 1) & 7) for i in range(3)])
     ready = mine
-    mine = doubled(doubled(mine, "x"), "zhi")
-    factor = inverse_factor(core.reshape(1), mine, swap(mine, "core"))
+    mine = exchange(copies(mine, 4), "zhi")
+    mine = exchange(copies(mine, 4), "x")
+    other = swap(mine, "core")
+    factor = inverse_factor(core.reshape(1), mine, other)
 
     low, high = by_slot[:, :, 0].reshape(64, 128), by_slot[:, :, 1].reshape(64, 128)
     upper = row >= 8
-    piece_a = lax.ppermute(jnp.where(upper, high, low), EVERY, spread_pairs(False))
-    piece_b = lax.ppermute(jnp.where(upper, low, high), EVERY, spread_pairs(True))
+    send_a = after(jnp.where(upper, high, low), placed)
+    send_b = after(jnp.where(upper, low, high), placed)
+    piece_a = lax.ppermute(send_a, EVERY, spread_pairs(False))
+    piece_b = lax.ppermute(send_b, EVERY, spread_pairs(True))
     pieces = jnp.stack([jnp.where(upper, piece_b, piece_a), jnp.where(upper, piece_a, piece_b)])
-    pieces = ordered_pair(pieces, swap(pieces, "zlo"), zlo).reshape(256, 128)
-    pieces = lax.optimization_barrier((pieces, ready))[0]
+    pieces = after(pieces, ready)
+    other = swap(pieces, "zlo")
+    pieces = ordered_pair(pieces, other, zlo).reshape(256, 128)
+    pieces = after(pieces, mine)
     pieces = exchange(copies(pieces, 8), "y").reshape(4, 2, 256, 128)
-
-    across = lax.optimization_barrier((doubled(chunk, "x"), pieces))[0]
-    across = exchange(copies(across, 4), "zhi")
+    other = swap(pieces, "core")
+
+    across = doubled(after(chunk, ready), "zhi")
+    across = after(across, pieces)
+    across = exchange(copies(across, 4), "x")
 
     hits = [jnp.int32(-1), jnp.int32(-1)]
     for i in range(2):
         for s in range(2):
             hits[i] = jnp.where(target[s] == i * 32 + blk, s, hits[i])
     info = jnp.stack([core, hits[0], hits[1]]).astype(jnp.int32)
-    result = update(info, working, pieces, swap(pieces, "core"), across, factor)
+    result = update(info, working, pieces, other, across, factor)
     return result.reshape(1024, 2, 1, 256)
 
 
 def solution(mesh):
     fine = Mesh(mesh.devices.reshape(2, 8, 2, 4, 4), EVERY)
     spec = P(ROWS, None, ("zlo", "y", "core"), None)
-    return jax.shard_map(local, mesh=fine, in_specs=(spec, P()), out_specs=spec, check_vma=False)
+    return jax.shard_map(sections, mesh=fine, in_specs=(spec, P()), out_specs=spec, check_vma=False)

time: 207 us -> 192 us (0.928)
  the two profiles are of different devices: /device:TPU:65 before, /device:TPU:1 now
where the time goes in v2:
time: 192 us; the launch traced here: 191 us
  starting transfers between devices  83.3 us (43%)
  waiting for transfers between devices  50.7 us (26%)
  Pallas kernels  34.2 us (18%)
  between operations  11.3 us (6%)
  local copies, waits for them, and re-layouts  9.22 us (5%)
  other arithmetic  2.65 us (1%)
    all_to_all x7, starting transfers between devices, exchange(): return lax.all_to_all(array, axis, 0, 0, tiled=True)  55.6 us
    all_to_all x7, waiting for transfers between devices, exchange(): return lax.all_to_all(array, axis, 0, 0, tiled=True)  44.5 us
    pallas_call x1, Pallas kernels, inverse_factor(): pl.pallas_call(factor_kernel, out_shape=jax.ShapeDtypeStruct((n, n), jnp....  21.6 us
    ppermute x5, starting transfers between devices, swap(): return lax.ppermute(array, axis, [(0, 1), (1, 0)])  19.6 us
    pallas_call x1, Pallas kernels, update(): pl.pallas_call(update_kernel, out_shape=jax.ShapeDtypeStruct(working.shap...  12.6 us
    broadcast_in_dim x5, local copies, waits for them, and re-layouts, copies(): return jnp.broadcast_to(array, (count, *array.shape))  4.31 us
    ppermute x1, waiting for transfers between devices, doubled(): near = lax.ppermute(array, axis, [(i, i ^ 1) for i in range(4)])  4.28 us
  transfers between devices with their start and end apart: 16, of which 8 were waited for; matrix products, arithmetic and copies ran while one was open for 1% of the time, Pallas kernels for 11%

profile of v2, /device:TPU:1, one launch (start us, length us, event | category | flops | bytes accessed | tf_op | source)
XLA Modules:
  0.0 191.2 jit_solution(13434310380569013628)
XLA Ops:
  5.1 4.8 %all-to-all-start = ((f32[4,4,2,64,128]{4,3,1,2,0:T(8,128)}), f32[4,4,2,64,128]{4,3,1,2,0:T(8,128)S(1)}, u32[]{:S(2)}, u32[]{:S(2)}) async-start(f32[4,4,2,64,128]{4,3,1,2,0:T(8,128)} %pad_maximum_fusion), calls=%async_computation | async-start | bytes 2097152 | tf_op jit(solution)/shard_map/all_to_all | solution.py:228
  11.3 8.4 %all-to-all-done = f32[4,4,2,64,128]{4,3,1,2,0:T(8,128)S(1)} async-done(((f32[4,4,2,64,128]{4,3,1,2,0:T(8,128)}), f32[4,4,2,64,128]{4,3,1,2,0:T(8,128)S(1)}, u32[]{:S(2)}, u32[]{:S(2)}) %all-to-all-start) | async-done | bytes 1048608 | tf_op jit(solution)/shard_map/all_to_all | solution.py:228
  20.5 14.5 %all-to-all-start.1 = ((f32[4,2,64,128]{3,2,1,0:T(8,128)}), f32[4,2,64,128]{3,2,1,0:T(8,128)S(1)}, u32[]{:S(2)}, u32[]{:S(2)}) async-start(f32[4,2,64,128]{3,2,1,0:T(8,128)} %pad_maximum_fusion.1), calls=%async_computation.1 | async-start | bytes 524288 | tf_op jit(solution)/shard_map/all_to_all | solution.py:228
  36.4 7.4 %all-to-all-done.1 = f32[4,2,64,128]{3,2,1,0:T(8,128)S(1)} async-done(((f32[4,2,64,128]{3,2,1,0:T(8,128)}), f32[4,2,64,128]{3,2,1,0:T(8,128)S(1)}, u32[]{:S(2)}, u32[]{:S(2)}) %all-to-all-start.1) | async-done | bytes 262176 | tf_op jit(solution)/shard_map/all_to_all | solution.py:228
  43.9 5.0 %collective-permute-start = (f32[3,16,128]{2,1,0:T(8,128)S(1)}, f32[3,16,128]{2,1,0:T(8,128)S(1)}, u32[]{:S(2)}, u32[]{:S(2)}) collective-permute-start(f32[3,16,128]{2,1,0:T(8,128)S(1)} %dynamic-slice_bitcast_fusion.2), channel_id=1, source_target_pairs={{0,16},{16,0},{1,17},{17,1},{2,18},{18,2},{3,19},{19,3},{4,20},{20... | collective-permute-start | bytes 73736 | tf_op jit(solution)/shard_map/ppermute | solution.py:199
  50.3 3.5 %collective-permute-start.1 = (f32[3,16,128]{2,1,0:T(8,128)S(1)}, f32[3,16,128]{2,1,0:T(8,128)S(1)}, u32[]{:S(2)}, u32[]{:S(2)}) collective-permute-start(f32[3,16,128]{2,1,0:T(8,128)S(1)} %pad_maximum_fusion.9), channel_id=1, source_target_pairs={{0,256},{256,0},{1,257},{257,1},{2,258},{258,2},{3,259},{259,3},{4... | collective-permute-start | bytes 73736 | tf_op jit(solution)/shard_map/ppermute | solution.py:199
  55.9 6.8 %all-to-all-start.2 = ((f32[8,3,16,128]{3,2,1,0:T(8,128)}), f32[8,3,16,128]{3,2,1,0:T(8,128)S(1)}, u32[]{:S(2)}, u32[]{:S(2)}) async-start(f32[8,3,16,128]{3,2,1,0:T(8,128)} %broadcast_in_dim.15), calls=%async_computation.2 | async-start | bytes 393216 | tf_op jit(solution)/shard_map/all_to_all | solution.py:228
  62.8 2.3 %collective-permute-start.2 = (f32[64,128]{1,0:T(8,128)S(1)}, f32[64,128]{1,0:T(8,128)S(1)}, u32[]{:S(2)}, u32[]{:S(2)}) collective-permute-start(f32[64,128]{1,0:T(8,128)S(1)} %bitcast.81), channel_id=1, source_target_pairs={{0,8},{1,72},{2,136},{3,200},{4,264},{5,328},{6,392},{7,456},{8,0}... | collective-permute-start | bytes 98312 | tf_op jit(solution)/shard_map/ppermute | solution.py:285
  69.0 2.7 %all-to-all-done.2 = f32[8,3,16,128]{3,2,1,0:T(8,128)S(1)} async-done(((f32[8,3,16,128]{3,2,1,0:T(8,128)}), f32[8,3,16,128]{3,2,1,0:T(8,128)S(1)}, u32[]{:S(2)}, u32[]{:S(2)}) %all-to-all-start.2) | async-done | bytes 196640 | tf_op jit(solution)/shard_map/all_to_all | solution.py:228
  72.4 18.2 %all-to-all-start.3 = ((f32[4,3,16,128]{3,2,1,0:T(8,128)}), f32[4,3,16,128]{3,2,1,0:T(8,128)S(1)}, u32[]{:S(2)}, u32[]{:S(2)}) async-start(f32[4,3,16,128]{3,2,1,0:T(8,128)} %broadcast_in_dim.16), calls=%async_computation.3 | async-start | bytes 196608 | tf_op jit(solution)/shard_map/all_to_all | solution.py:228
  90.6 2.7 %collective-permute-start.4 = (f32[2,64,128]{2,1,0:T(8,128)S(1)}, f32[2,64,128]{2,1,0:T(8,128)S(1)}, u32[]{:S(2)}, u32[]{:S(2)}) collective-permute-start(f32[2,64,128]{2,1,0:T(8,128)S(1)} %pad_maximum_fusion.5), channel_id=1, source_target_pairs={{0,256},{256,0},{1,257},{257,1},{2,258},{258,2},{3,259},{259,3},{4... | collective-permute-start | bytes 196616 | tf_op jit(solution)/shard_map/ppermute | solution.py:199
  93.4 4.3 %all-to-all-done.3 = f32[4,3,16,128]{3,2,1,0:T(8,128)S(1)} async-done(((f32[4,3,16,128]{3,2,1,0:T(8,128)}), f32[4,3,16,128]{3,2,1,0:T(8,128)S(1)}, u32[]{:S(2)}, u32[]{:S(2)}) %all-to-all-start.3) | async-done | bytes 98336 | tf_op jit(solution)/shard_map/all_to_all | solution.py:228
  98.5 4.1 %all-to-all-start.4 = ((f32[4,4,3,16,128]{4,3,2,1,0:T(8,128)}), f32[4,4,3,16,128]{4,3,2,1,0:T(8,128)S(1)}, u32[]{:S(2)}, u32[]{:S(2)}) async-start(f32[4,4,3,16,128]{4,3,2,1,0:T(8,128)} %broadcast_in_dim.17), calls=%async_computation.4 | async-start | bytes 786432 | tf_op jit(solution)/shard_map/all_to_all | solution.py:228
  102.6 6.2 %all-to-all-done.4.own_ref = f32[4,4,3,16,128]{4,3,2,1,0:T(8,128)S(1)} async-done(((f32[4,4,3,16,128]{4,3,2,1,0:T(8,128)}), f32[4,4,3,16,128]{4,3,2,1,0:T(8,128)S(1)}, u32[]{:S(2)}, u32[]{:S(2)}) %all-to-all-start.4) | async-done | bytes 393248 | tf_op jit(solution)/shard_map/all_to_all | solution.py:228
  109.9 3.6 %all-to-all-start.5 = ((f32[8,256,128]{2,1,0:T(8,128)}), f32[8,256,128]{2,1,0:T(8,128)S(1)}, u32[]{:S(2)}, u32[]{:S(2)}) async-start(f32[8,256,128]{2,1,0:T(8,128)} %broadcast_in_dim.18), calls=%async_computation.5 | async-start | bytes 2097152 | tf_op jit(solution)/shard_map/all_to_all | solution.py:228
  113.6 2.3 %collective-permute-start.6 = (f32[2,64,128]{2,1,0:T(8,128)S(1)}, f32[2,64,128]{2,1,0:T(8,128)S(1)}, u32[]{:S(2)}, u32[]{:S(2)}) collective-permute-start(f32[2,64,128]{2,1,0:T(8,128)S(1)} %pad_maximum_fusion.6), channel_id=1, source_target_pairs={{0,1},{1,0},{2,3},{3,2},{4,5},{5,4},{6,7},{7,6},{8,9},{9,8},{10,11... | collective-permute-start | bytes 196616 | tf_op jit(solution)/shard_map/ppermute | solution.py:237
  115.9 4.3 %collective-permute-done.6 = f32[2,64,128]{2,1,0:T(8,128)S(1)} collective-permute-done((f32[2,64,128]{2,1,0:T(8,128)S(1)}, f32[2,64,128]{2,1,0:T(8,128)S(1)}, u32[]{:S(2)}, u32[]{:S(2)}) %collective-permute-start.6) | collective-permute-done | bytes 65568 | tf_op jit(solution)/shard_map/ppermute | solution.py:237
  120.2 2.9 %collective-permute-start.7 = (f32[2,2,64,128]{3,2,1,0:T(8,128)S(1)}, f32[2,2,64,128]{3,2,1,0:T(8,128)S(1)}, u32[]{:S(2)}, u32[]{:S(2)}) collective-permute-start(f32[2,2,64,128]{3,2,1,0:T(8,128)S(1)} %pad_maximum_fusion.4), channel_id=1, source_target_pairs={{0,2},{1,3},{2,0},{3,1},{4,6},{5,7},{6,4},{7,5},{8,10},{9,11},{10,... | collective-permute-start | bytes 393224 | tf_op jit(solution)/shard_map/ppermute | solution.py:239
  123.1 15.5 %all-to-all-done.5 = f32[8,256,128]{2,1,0:T(8,128)S(1)} async-done(((f32[8,256,128]{2,1,0:T(8,128)}), f32[8,256,128]{2,1,0:T(8,128)S(1)}, u32[]{:S(2)}, u32[]{:S(2)}) %all-to-all-start.5) | async-done | bytes 1048608 | tf_op jit(solution)/shard_map/all_to_all | solution.py:228
  138.6 6.4 %collective-permute-start.5 = (f32[4,2,256,128]{3,2,1,0:T(8,128)S(1)}, f32[4,2,256,128]{3,2,1,0:T(8,128)S(1)}, u32[]{:S(2)}, u32[]{:S(2)}) collective-permute-start(f32[4,2,256,128]{3,2,1,0:T(8,128)S(1)} %bitcast.67), channel_id=1, source_target_pairs={{0,16},{16,0},{1,17},{17,1},{2,18},{18,2},{3,19},{19,3},{4,20},{20... | collective-permute-start | bytes 3145736 | tf_op jit(solution)/shard_map/ppermute | solution.py:199
  146.2 3.5 %all-to-all-start.6 = ((f32[4,4,2,64,128]{4,3,2,1,0:T(8,128)}), f32[4,4,2,64,128]{4,3,2,1,0:T(8,128)S(1)}, u32[]{:S(2)}, u32[]{:S(2)}) async-start(f32[4,4,2,64,128]{4,3,2,1,0:T(8,128)} %broadcast_in_dim.19), calls=%async_computation.6 | async-start | bytes 2097152 | tf_op jit(solution)/shard_map/all_to_all | solution.py:228
  149.8 1.9 %collective-permute-start.8 = (f32[4,4,3,16,128]{4,3,2,1,0:T(8,128)S(1)}, f32[4,4,3,16,128]{4,3,2,1,0:T(8,128)}, u32[]{:S(2)}, u32[]{:S(2)}) collective-permute-start(f32[4,4,3,16,128]{4,3,2,1,0:T(8,128)S(1)} %all-to-all-done.4.own_ref), channel_id=1, source_target_pairs={{0,16},{16,0},{1,17},{17,1},{2,18},{18,2},{3,19},{19,3},{4,20},{20... | collective-permute-start | bytes 1179656 | tf_op jit(solution)/shard_map/ppermute | solution.py:199
  155.1 21.6 %shard_map.28.g_ref = f32[512,512]{1,0:T(8,128)} custom-call(s32[1]{0:T(128)} %bitcast.core_ref, f32[4,4,3,16,128]{4,3,2,1,0:T(8,128)} %copy-done.3, f32[4,4,3,16,128]{4,3,2,1,0:T(8,128)} %collective-permute-done.8.other_ref), custom_call_target="tpu_custom_call" | custom-call | flops 2147483648 | bytes 2097152 | tf_op jit(solution)/shard_map/pallas_call | solution.py:106
  178.6 12.6 %shard_map.29 = f32[4096,128]{1,0:T(8,128)} custom-call(s32[3]{0:T(128)} %pad_add_fusion.info_ref, f32[4096,128]{1,0:T(8,128)} %bitcast.66, f32[4,2,256,128]{3,2,1,0:T(8,128)} %bitcast.68, f32[4,2,256,128]{3,2,1,0:T(8,128)} %copy-done.2, f32[4,4,2,64,128]{4,3,2,1,0:T(8,128)} %copy-done.1, f32[512,512]{1,0:T(8,128)} %shard_map.28.g_ref), custom_call_target="tpu_custom_call" | custom-call | flops 1073741824 | bytes 8388608 | tf_op jit(solution)/shard_map/pallas_call | solution.py:184
  (58 shorter events, 14.4 us)
Async XLA Ops:
  5.1 14.6 %all-to-all-start = ((f32[4,4,2,64,128]{4,3,1,2,0:T(8,128)}), f32[4,4,2,64,128]{4,3,1,2,0:T(8,128)S(1)}, u32[]{:S(2)}, u32[]{:S(2)}) async-start(f32[4,4,2,64,128]{4,3,1,2,0:T(8,128)} %pad_maximum_fusion), calls=%async_computation | async-start | bytes 2097152 | tf_op jit(solution)/shard_map/all_to_all | solution.py:228
  20.5 23.3 %all-to-all-start.1 = ((f32[4,2,64,128]{3,2,1,0:T(8,128)}), f32[4,2,64,128]{3,2,1,0:T(8,128)S(1)}, u32[]{:S(2)}, u32[]{:S(2)}) async-start(f32[4,2,64,128]{3,2,1,0:T(8,128)} %pad_maximum_fusion.1), calls=%async_computation.1 | async-start | bytes 524288 | tf_op jit(solution)/shard_map/all_to_all | solution.py:228
  43.9 6.4 %collective-permute-start = (f32[3,16,128]{2,1,0:T(8,128)S(1)}, f32[3,16,128]{2,1,0:T(8,128)S(1)}, u32[]{:S(2)}, u32[]{:S(2)}) collective-permute-start(f32[3,16,128]{2,1,0:T(8,128)S(1)} %dynamic-slice_bitcast_fusion.2), channel_id=1, source_target_pairs={{0,16},{16,0},{1,17},{17,1},{2,18},{18,2},{3,19},{19,3},{4,20},{20... | collective-permute-start | bytes 73736 | tf_op jit(solution)/shard_map/ppermute | solution.py:199
  50.3 4.9 %collective-permute-start.1 = (f32[3,16,128]{2,1,0:T(8,128)S(1)}, f32[3,16,128]{2,1,0:T(8,128)S(1)}, u32[]{:S(2)}, u32[]{:S(2)}) collective-permute-start(f32[3,16,128]{2,1,0:T(8,128)S(1)} %pad_maximum_fusion.9), channel_id=1, source_target_pairs={{0,256},{256,0},{1,257},{257,1},{2,258},{258,2},{3,259},{259,3},{4... | collective-permute-start | bytes 73736 | tf_op jit(solution)/shard_map/ppermute | solution.py:199
  55.9 15.8 %all-to-all-start.2 = ((f32[8,3,16,128]{3,2,1,0:T(8,128)}), f32[8,3,16,128]{3,2,1,0:T(8,128)S(1)}, u32[]{:S(2)}, u32[]{:S(2)}) async-start(f32[8,3,16,128]{3,2,1,0:T(8,128)} %broadcast_in_dim.15), calls=%async_computation.2 | async-start | bytes 393216 | tf_op jit(solution)/shard_map/all_to_all | solution.py:228
  62.8 6.2 %collective-permute-start.2 = (f32[64,128]{1,0:T(8,128)S(1)}, f32[64,128]{1,0:T(8,128)S(1)}, u32[]{:S(2)}, u32[]{:S(2)}) collective-permute-start(f32[64,128]{1,0:T(8,128)S(1)} %bitcast.81), channel_id=1, source_target_pairs={{0,8},{1,72},{2,136},{3,200},{4,264},{5,328},{6,392},{7,456},{8,0}... | collective-permute-start | bytes 98312 | tf_op jit(solution)/shard_map/ppermute | solution.py:285
  65.1 3.9 %collective-permute-start.3 = (f32[64,128]{1,0:T(8,128)S(1)}, f32[64,128]{1,0:T(8,128)S(1)}, u32[]{:S(2)}, u32[]{:S(2)}) collective-permute-start(f32[64,128]{1,0:T(8,128)S(1)} %bitcast.80), channel_id=1, source_target_pairs={{0,0},{1,64},{2,128},{3,192},{4,256},{5,320},{6,384},{7,448},{8,8}... | collective-permute-start | bytes 98312 | tf_op jit(solution)/shard_map/ppermute | solution.py:284
  72.4 25.2 %all-to-all-start.3 = ((f32[4,3,16,128]{3,2,1,0:T(8,128)}), f32[4,3,16,128]{3,2,1,0:T(8,128)S(1)}, u32[]{:S(2)}, u32[]{:S(2)}) async-start(f32[4,3,16,128]{3,2,1,0:T(8,128)} %broadcast_in_dim.16), calls=%async_computation.3 | async-start | bytes 196608 | tf_op jit(solution)/shard_map/all_to_all | solution.py:228
  90.6 12.0 %collective-permute-start.4 = (f32[2,64,128]{2,1,0:T(8,128)S(1)}, f32[2,64,128]{2,1,0:T(8,128)S(1)}, u32[]{:S(2)}, u32[]{:S(2)}) collective-permute-start(f32[2,64,128]{2,1,0:T(8,128)S(1)} %pad_maximum_fusion.5), channel_id=1, source_target_pairs={{0,256},{256,0},{1,257},{257,1},{2,258},{258,2},{3,259},{259,3},{4... | collective-permute-start | bytes 196616 | tf_op jit(solution)/shard_map/ppermute | solution.py:199
  98.5 10.4 %all-to-all-start.4 = ((f32[4,4,3,16,128]{4,3,2,1,0:T(8,128)}), f32[4,4,3,16,128]{4,3,2,1,0:T(8,128)S(1)}, u32[]{:S(2)}, u32[]{:S(2)}) async-start(f32[4,4,3,16,128]{4,3,2,1,0:T(8,128)} %broadcast_in_dim.17), calls=%async_computation.4 | async-start | bytes 786432 | tf_op jit(solution)/shard_map/all_to_all | solution.py:228
  108.8 40.9 %copy-start.3 = (f32[4,4,3,16,128]{4,3,2,1,0:T(8,128)}, f32[4,4,3,16,128]{4,3,2,1,0:T(8,128)S(1)}, u32[]{:S(2)}) copy-start(f32[4,4,3,16,128]{4,3,2,1,0:T(8,128)S(1)} %all-to-all-done.4.own_ref) | copy-start | bytes 1179652
  109.9 28.7 %all-to-all-start.5 = ((f32[8,256,128]{2,1,0:T(8,128)}), f32[8,256,128]{2,1,0:T(8,128)S(1)}, u32[]{:S(2)}, u32[]{:S(2)}) async-start(f32[8,256,128]{2,1,0:T(8,128)} %broadcast_in_dim.18), calls=%async_computation.5 | async-start | bytes 2097152 | tf_op jit(solution)/shard_map/all_to_all | solution.py:228
  113.6 6.6 %collective-permute-start.6 = (f32[2,64,128]{2,1,0:T(8,128)S(1)}, f32[2,64,128]{2,1,0:T(8,128)S(1)}, u32[]{:S(2)}, u32[]{:S(2)}) collective-permute-start(f32[2,64,128]{2,1,0:T(8,128)S(1)} %pad_maximum_fusion.6), channel_id=1, source_target_pairs={{0,1},{1,0},{2,3},{3,2},{4,5},{5,4},{6,7},{7,6},{8,9},{9,8},{10,11... | collective-permute-start | bytes 196616 | tf_op jit(solution)/shard_map/ppermute | solution.py:237
  120.2 24.9 %collective-permute-start.7 = (f32[2,2,64,128]{3,2,1,0:T(8,128)S(1)}, f32[2,2,64,128]{3,2,1,0:T(8,128)S(1)}, u32[]{:S(2)}, u32[]{:S(2)}) collective-permute-start(f32[2,2,64,128]{3,2,1,0:T(8,128)S(1)} %pad_maximum_fusion.4), channel_id=1, source_target_pairs={{0,2},{1,3},{2,0},{3,1},{4,6},{5,7},{6,4},{7,5},{8,10},{9,11},{10,... | collective-permute-start | bytes 393224 | tf_op jit(solution)/shard_map/ppermute | solution.py:239
  138.6 7.6 %copy-start = (f32[8,256,128]{2,1,0:T(8,128)}, f32[8,256,128]{2,1,0:T(8,128)S(1)}, u32[]{:S(2)}) copy-start(f32[8,256,128]{2,1,0:T(8,128)S(1)} %all-to-all-done.5) | copy-start | bytes 3145732
  138.6 38.0 %collective-permute-start.5 = (f32[4,2,256,128]{3,2,1,0:T(8,128)S(1)}, f32[4,2,256,128]{3,2,1,0:T(8,128)S(1)}, u32[]{:S(2)}, u32[]{:S(2)}) collective-permute-start(f32[4,2,256,128]{3,2,1,0:T(8,128)S(1)} %bitcast.67), channel_id=1, source_target_pairs={{0,16},{16,0},{1,17},{17,1},{2,18},{18,2},{3,19},{19,3},{4,20},{20... | collective-permute-start | bytes 3145736 | tf_op jit(solution)/shard_map/ppermute | solution.py:199
  146.2 30.4 %all-to-all-start.6 = ((f32[4,4,2,64,128]{4,3,2,1,0:T(8,128)}), f32[4,4,2,64,128]{4,3,2,1,0:T(8,128)S(1)}, u32[]{:S(2)}, u32[]{:S(2)}) async-start(f32[4,4,2,64,128]{4,3,2,1,0:T(8,128)} %broadcast_in_dim.19), calls=%async_computation.6 | async-start | bytes 2097152 | tf_op jit(solution)/shard_map/all_to_all | solution.py:228
  149.8 5.3 %collective-permute-start.8 = (f32[4,4,3,16,128]{4,3,2,1,0:T(8,128)S(1)}, f32[4,4,3,16,128]{4,3,2,1,0:T(8,128)}, u32[]{:S(2)}, u32[]{:S(2)}) collective-permute-start(f32[4,4,3,16,128]{4,3,2,1,0:T(8,128)S(1)} %all-to-all-done.4.own_ref), channel_id=1, source_target_pairs={{0,16},{16,0},{1,17},{17,1},{2,18},{18,2},{3,19},{19,3},{4,20},{20... | collective-permute-start | bytes 1179656 | tf_op jit(solution)/shard_map/ppermute | solution.py:199
  176.6 1.0 copy-start.1
  177.7 1.0 copy-start.2
